TPU v7x, 32 devices: a whole 2x2x4 slice. The times are simulated.
32 devices in a mesh: seg: 4 (over y, core), sub: 8 (over z, x).
Axes of the slice: x: 2, y: 2, z: 4, core: 2. Of those that a mesh axis runs over, the one named last changes fastest.
Arguments:
- nodal_loads: float32 [4, 8, 32, 3072], P('seg', 'sub'), may hold values from -6 to 6
- schur_matrix: bfloat16 [4, 8, 3072, 3072], P('seg', 'sub'), may hold values from -2 to 9, as said below
- face_rows: int32 [4, 8, 3072], P('seg', 'sub'), may hold values from 0 to 3071, each once within a row
- face_len: int32 [4, 8, 2], replicated, may hold values from 192 to 768, as said below
- relax_step: float32 [4, 8], P('seg', 'sub'), may hold values from 0.03 to 0.1
- coarse_basis: float32 [4, 8, 4, 3072], P('seg', 'sub'), may hold values from -0.625 to 0.625
- primal_index: int32 [4, 8, 4], replicated, may hold values from 0 to 71, as said below
- coarse_inverse: float32 [72, 72], replicated, may hold values from -1 to 1.5, as said below
Outputs:
- solution: float32 [4, 8, 32, 3072], P('seg', 'sub')
- residual: float32 [4, 8, 32, 3072], P('seg', 'sub')
Inputs may be any that keep to these rules, and one draw needn't show every extreme that they name: `schur_matrix`: symmetric in its last two dimensions and positive definite for each subdomain. `face_len`: entry [s, j, 0] counts the shared slots of the face between subdomains j and (j+1) mod 8 of segment s; entry [s, j, 1] those of the face between segments s and s+1 at subdomain j (not read for the last segment). Some entry [s, j, 0] equals 768. `primal_index`: one global number for each face: the face between subdomains j and (j+1) mod 8 of segment s, and the face below segment s at subdomain j (and above the last segment), numbered in a random order. Subdomains sharing a face name the same number; a face at the bridge's ends belongs to one subdomain only. `coarse_inverse`: symmetric positive definite.
All inputs are finite; a program needn't handle non-finite values.
Results may differ from a plain program's by a relative error of at most 0.0015.
Values sent between devices are 32-bit elements; how exact they have to be, the bound alone decides.
A program may use at most 128 MiB of HBM per device.

v0:
```python
import functools

import jax
import jax.numpy as jnp
from jax import lax
from jax.experimental import pallas as pl
from jax.experimental.pallas import tpu as pltpu
from jax.sharding import PartitionSpec as P

DEG = 3
ITERS = 3

HIGH = lax.Precision.HIGHEST
MESH = pl.DeviceIdType.MESH
LANES = 128
ROWS = 8
F32 = jnp.float32
BF16 = jnp.bfloat16

NN = (((1,), (0,)), ((), ()))
NT = (((1,), (1,)), ((), ()))


def split(values):
    upper = values.astype(BF16)
    return upper, (values - upper.astype(F32)).astype(BF16)


def small(left, right, dims=NN):
    return lax.dot_general(left, right, dims, precision=HIGH, preferred_element_type=F32)


def solve_kernel(
    counts,
    face_len,
    primal,
    relax_ref,
    loads,
    schur,
    rows_ref,
    basis_ref,
    coarse_ref,
    solution,
    residual,
    matrix,
    lhs,
    rights,
    weighted,
    scaled,
    state,
    fresh,
    precond,
    direction,
    image,
    weight,
    place_lane,
    place_tile,
    back_lane,
    back_tile,
    coarse_rows,
    face_hot,
    small_state,
    outgoing,
    incoming,
    coarse_first,
    coarse_second,
    inner_first,
    inner_second,
    load_sems,
    halo_sems,
    coarse_first_sems,
    coarse_second_sems,
    inner_first_sems,
    inner_second_sems,
):
    block, width = loads.shape[2:]
    tiles = width // LANES
    face_tiles = tiles // 4
    groups = block // ROWS
    places = {axis: lax.axis_index(axis) for axis in counts}
    chunks = load_sems.shape[0]
    chunk = width // chunks

    def peer(axis, shift):
        return lax.rem(places[axis] + (shift + counts[axis]) % counts[axis], counts[axis])

    fetches = []
    for i in range(chunks):
        rows = pl.ds(i * chunk, chunk)
        fetch = pltpu.make_async_copy(schur.at[0, 0, rows], matrix.at[rows], load_sems.at[i])
        fetch.start()
        fetches.append(fetch)

    barrier = pltpu.get_barrier_semaphore()
    greeted = [{axis: peer(axis, d)} for axis in counts for d in range(1, counts[axis])]
    for target in greeted:
        pl.semaphore_signal(barrier, inc=1, device_id=target, device_id_type=MESH)

    slot_rows = rows_ref[0]
    row_tile = slot_rows >> 7
    row_lane = slot_rows & (LANES - 1)
    for d in range(tiles):
        columns = slice(d * LANES, (d + 1) * LANES)
        place_tile[d : d + 1] = row_tile[:, columns]
        place_lane[d : d + 1] = row_lane[:, columns]

    def gathered(read, lane_ref, tile_ref, d):
        lane = jnp.broadcast_to(lane_ref[pl.ds(d, 1)], (ROWS, LANES))
        tile = jnp.broadcast_to(tile_ref[pl.ds(d, 1)], (ROWS, LANES))
        parts = [jnp.zeros((ROWS, LANES), F32) for _ in range(groups)]
        for s in range(tiles):
            hit = tile == s
            for g in range(groups):
                moved = jnp.take_along_axis(
                    read(s, g), lane, axis=1, mode="promise_in_bounds"
                )
                parts[g] = jnp.where(hit, moved, parts[g])
        return jnp.concatenate(parts, axis=0)

    def pairs(count, visit):
        unroll = 2 if count % 2 == 0 else 1

        def step(i, _):
            for u in range(unroll):
                visit(i * unroll + u)
            return 0

        lax.fori_loop(0, count // unroll, step, 0)

    def part(g):
        return slice(g * ROWS, (g + 1) * ROWS)

    def span(d):
        return pl.ds(pl.multiple_of(d * LANES, LANES), LANES)

    routes = (
        (1, 0, {"sub": peer("sub", 1)}),
        (0, 1, {"sub": peer("sub", -1)}),
        (3, 2, {"seg": peer("seg", 1)}),
        (2, 3, {"seg": peer("seg", -1)}),
    )

    def halo_copies(e):
        return [
            pltpu.make_async_remote_copy(
                src_ref=outgoing.at[e, face],
                dst_ref=incoming.at[e, landing],
                send_sem=halo_sems.at[e, 0, landing],
                recv_sem=halo_sems.at[e, 1, landing],
                device_id=target,
                device_id_type=MESH,
            )
            for face, landing, target in routes
        ]

    def halo_start(e, read):
        copies = halo_copies(e)
        for (face, _, _), copy in zip(routes, copies):

            def visit(d, face=face):
                outgoing[e, face, :, span(d)] = gathered(
                    read, place_lane, place_tile, d + face * face_tiles
                )

            pairs(face_tiles, visit)
            copy.start()

    def halo_wait(e):
        for copy in halo_copies(e):
            copy.wait()

    def halo_add(e, visit):
        def read(s, g):
            at = (s % face_tiles) * LANES
            return incoming[e, s // face_tiles, part(g), at : at + LANES]

        def tile(d):
            visit(span(d), gathered(read, back_lane, back_tile, d))

        pairs(tiles, tile)

    def sum_copy(axis, held, sems, r, d, landing):
        own = held.at[r, places[axis]]
        return pltpu.make_async_remote_copy(
            src_ref=own,
            dst_ref=held.at[r, peer(axis, -d)] if landing else own,
            send_sem=sems.at[r, 0, d],
            recv_sem=sems.at[r, 1, d],
            device_id={axis: peer(axis, d)},
            device_id_type=MESH,
        )

    def sum_start(axis, held, sems, r, value):
        held[r, places[axis]] = value
        for d in range(1, counts[axis]):
            sum_copy(axis, held, sems, r, d, False).start()

    def sum_finish(axis, held, sems, r):
        for d in range(1, counts[axis]):
            sum_copy(axis, held, sems, r, d, True).wait_recv()
        for d in range(1, counts[axis]):
            sum_copy(axis, held, sems, r, d, False).wait_send()
        value = held[r, 0]
        for i in range(1, counts[axis]):
            value = value + held[r, i]
        return value

    def product(source, visit):
        step = width // 2

        def column(j, _):
            columns = pl.ds(pl.multiple_of(j * step, step), step)
            both = jnp.dot(source[...], matrix[:, columns], preferred_element_type=F32)
            visit(columns, both[:block] + both[block:])
            return 0

        lax.fori_loop(0, 2, column, 0)

    def put_split(target, columns, values):
        upper, lower = split(values)
        target[:block, columns] = upper
        target[block:, columns] = lower

    everything = slice(0, width)

    pl.semaphore_wait(barrier, len(greeted))
    halo_start(0, lambda s, g: loads[0, 0, part(g), s * LANES : (s + 1) * LANES])

    padded_tiles = -(-tiles // 16) * 16
    at = lax.broadcasted_iota(jnp.int32, (padded_tiles, width), 0)
    slot = lax.broadcasted_iota(jnp.int32, (padded_tiles, width), 1)
    here = at == row_tile
    high_slot = jnp.where(here, slot >> 6, 0).astype(F32).astype(BF16)
    low_slot = jnp.where(here, slot & 63, 0).astype(F32).astype(BF16)
    lane_hot = (
        jnp.where(lax.broadcasted_iota(jnp.int32, (LANES, width), 0) == row_lane, 1.0, 0.0)
    ).astype(BF16)
    found = lax.dot_general(
        jnp.concatenate([high_slot, low_slot], axis=0),
        lane_hot,
        NT,
        preferred_element_type=F32,
    )
    back = (64.0 * found[:padded_tiles] + found[padded_tiles:]).astype(jnp.int32)[:tiles]
    seg_at, sub_at = places["seg"], places["sub"]
    seg_below = jnp.maximum(seg_at - 1, 0)
    lengths = (
        face_len[seg_at, peer("sub", -1), 0],
        face_len[seg_at, sub_at, 0],
        jnp.where(seg_at > 0, face_len[seg_below, sub_at, 1], 0),
        jnp.where(seg_at < counts["seg"] - 1, face_len[seg_at, sub_at, 1], 0),
    )
    face_width = width // 4
    live = jnp.zeros(back.shape, jnp.bool_)
    for f in range(4):
        inside = (back >= f * face_width) & (back < f * face_width + lengths[f])
        live = live | inside
    back_tile[...] = jnp.where(live, back >> 7, -1)
    back_lane[...] = back & (LANES - 1)
    weight_tiles = jnp.where(live, 0.5, 1.0)
    for d in range(tiles):
        weight[:, d * LANES : (d + 1) * LANES] = jnp.broadcast_to(
            weight_tiles[d : d + 1], (ROWS, LANES)
        )

    coarse_padded = coarse_rows.shape[1]
    lane_at = lax.broadcasted_iota(jnp.int32, (1, coarse_padded), 1)
    hot = jnp.concatenate(
        [jnp.where(lane_at == primal[seg_at, sub_at, f], 1.0, 0.0) for f in range(4)]
        + [jnp.zeros((ROWS - 4, coarse_padded), F32)],
        axis=0,
    )
    face_hot[...] = hot
    coarse_count = coarse_ref.shape[0]
    coarse_rows[...] = jnp.zeros_like(coarse_rows)
    coarse_rows[:, :coarse_count] = small(hot[:, :coarse_count], coarse_ref[...], NT)

    relax = relax_ref[0, 0]
    wide = (block, LANES)
    row_at = lax.broadcasted_iota(jnp.int32, wide, 0)
    column_at = lax.broadcasted_iota(jnp.int32, wide, 1)
    eye = jnp.where(row_at == column_at, 1.0, 0.0)[:, :block]

    def symmetric(matrix):
        return 0.5 * (matrix + small(eye, matrix, NT))

    def inverse(values):
        rows = row_at[:, :block]
        lanes = column_at[:, :block]
        for k in range(block):
            pivot = 1.0 / values[k : k + 1, k : k + 1]
            across = jnp.where(lanes[:1] == k, pivot, values[k : k + 1] * pivot)
            down = values[:, k : k + 1]
            values = jnp.where(
                rows == k, across, jnp.where(lanes == k, 0.0, values) - down * across
            )
        return values

    def mixed(left, right_ref):
        upper, lower = split(left)
        right_upper, right_lower = split(right_ref[...])
        both = jnp.dot(
            jnp.concatenate([upper, lower], axis=0), right_upper, preferred_element_type=F32
        )
        return both[:block] + both[block:] + jnp.dot(
            upper, right_lower, preferred_element_type=F32
        )

    direction[...] = jnp.zeros_like(direction)
    image[...] = jnp.zeros_like(image)
    solution[...] = jnp.zeros_like(solution)
    rights[...] = jnp.zeros_like(rights)
    small_state[...] = jnp.zeros_like(small_state)

    halo_wait(0)

    def first_residual(columns, moved):
        residual[0, 0, :, columns] = loads[0, 0, :, columns] + moved

    halo_add(0, first_residual)
    for fetch in fetches:
        fetch.wait()

    def round_of(r, _):
        every_weight = jnp.concatenate([weight[...]] * groups, axis=0)
        own_weighted = residual[0, 0] * every_weight
        weighted[...] = own_weighted
        own_scaled = relax * own_weighted
        scaled[...] = own_scaled
        state[...] = own_scaled
        put_split(lhs.at[0], everything, own_scaled)
        terms = jnp.zeros((block, coarse_padded), F32)
        for f in range(4):
            local = jnp.sum(own_weighted * basis_ref[0, 0, f : f + 1], axis=1, keepdims=True)
            terms = terms + local * face_hot[f : f + 1]
        sum_start("sub", coarse_first, coarse_first_sems, r, terms)

        coarse_sum = None
        for sweep in range(DEG):

            def relaxed(columns, moved, sweep=sweep):
                updated = scaled[:, columns] + state[:, columns] - relax * moved
                state[:, columns] = updated
                put_split(lhs.at[(sweep + 1) % 2], columns, updated)

            product(lhs.at[sweep % 2], relaxed)
            if sweep == 0:
                terms = sum_finish("sub", coarse_first, coarse_first_sems, r)
                sum_start("seg", coarse_second, coarse_second_sems, r, terms)
            if sweep == DEG - 1:
                coarse_sum = sum_finish("seg", coarse_second, coarse_second_sems, r)

        corrected = state[...]
        for f in range(4):
            picked = jnp.sum(coarse_sum * coarse_rows[f : f + 1], axis=1, keepdims=True)
            corrected = corrected + picked * basis_ref[0, 0, f : f + 1]
        state[...] = corrected * jnp.concatenate([weight[...]] * groups, axis=0)
        halo_start(1 + 2 * r, lambda s, g: state[part(g), s * LANES : (s + 1) * LANES])
        small_state[0] = inverse_or_zero(r)
        put_split(rights_view(0), everything, weighted[...])
        put_split(
            rights_view(2),
            everything,
            image[...] * jnp.concatenate([weight[...]] * groups, axis=0),
        )
        halo_wait(1 + 2 * r)

        def joined(columns, moved):
            values = state[:, columns] + moved
            precond[:, columns] = values
            put_split(lhs.at[0], columns, values)

        halo_add(1 + 2 * r, joined)

        def imaged(columns, moved):
            fresh[:, columns] = moved
            put_split(rights_view(1), columns, moved)

        product(lhs.at[0], imaged)
        left = lhs[0]
        both = lax.dot_general(left, rights[0], NT, preferred_element_type=F32)
        both = both + lax.dot_general(left, rights[1], NT, preferred_element_type=F32)
        sum_start("sub", inner_first, inner_first_sems, r, both[:block] + both[block:])
        halo_start(2 + 2 * r, lambda s, g: fresh[part(g), s * LANES : (s + 1) * LANES])
        terms = sum_finish("sub", inner_first, inner_first_sems, r)
        sum_start("seg", inner_second, inner_second_sems, r, terms)
        sums = sum_finish("seg", inner_second, inner_second_sems, r)
        rho = symmetric(sums[:, :block])
        own = pltpu.roll(sums, LANES - block, 1)[:, :block]
        cross = pltpu.roll(sums, LANES - 2 * block, 1)[:, :block]
        beta_t = small(rho, small_state[0])
        curvature = symmetric(
            own
            + 2.0 * small(cross, beta_t, NT)
            + small(small(beta_t, small_state[2]), beta_t, NT)
        )
        small_state[1] = rho
        small_state[2] = curvature
        alpha_t = small(rho, inverse(curvature))
        small_state[3] = beta_t
        small_state[4] = alpha_t
        direction[...] = precond[...] + mixed(beta_t, direction)
        solution[0, 0] = solution[0, 0] + mixed(alpha_t, direction)
        halo_wait(2 + 2 * r)
        turned = mixed(beta_t, image)
        image[...] = fresh[...] + turned

        def added(columns, moved):
            image[:, columns] = image[:, columns] + moved

        halo_add(2 + 2 * r, added)
        residual[0, 0] = residual[0, 0] - mixed(alpha_t, image)
        return 0

    def rights_view(i):
        return _Rights(rights, i, block)

    def inverse_or_zero(r):
        first = r == 0
        safe = jnp.where(first, eye, small_state[1])
        return jnp.where(first, 0.0, inverse(safe))

    lax.fori_loop(0, ITERS, round_of, 0)


class _Rights:
    def __init__(self, ref, at, block):
        self.ref, self.at, self.block = ref, at, block

    def __setitem__(self, key, value):
        rows, columns = key
        half = 0 if rows.start is None else 1
        self.ref[half, self.at * self.block : (self.at + 1) * self.block, columns] = value


def body(
    nodal_loads,
    schur_matrix,
    face_rows,
    face_len,
    relax_step,
    coarse_basis,
    primal_index,
    coarse_inverse,
):
    counts = {"sub": lax.axis_size("sub"), "seg": lax.axis_size("seg")}
    block, width = nodal_loads.shape[2:]
    tiles = width // LANES
    coarse_padded = -(-coarse_inverse.shape[0] // LANES) * LANES
    halos = 1 + 2 * ITERS
    plane = pltpu.VMEM((block, width), F32)
    index = pltpu.VMEM((tiles, LANES), jnp.int32)
    dma = pltpu.SemaphoreType.DMA

    def held(axis, columns):
        return pltpu.VMEM((ITERS, counts[axis], block, columns), F32)

    def held_sems(axis):
        return dma((ITERS, 2, counts[axis]))

    out = jax.ShapeDtypeStruct(nodal_loads.shape, F32)
    smem = pl.BlockSpec(memory_space=pltpu.SMEM)
    vmem = pl.BlockSpec(memory_space=pltpu.VMEM)
    return pl.pallas_call(
        functools.partial(solve_kernel, counts),
        out_shape=(out, out),
        in_specs=[
            smem,
            smem,
            smem,
            vmem,
            pl.BlockSpec(memory_space=pl.ANY),
            vmem,
            vmem,
            vmem,
        ],
        out_specs=(vmem, vmem),
        scratch_shapes=[
            pltpu.VMEM((width, width), BF16),
            pltpu.VMEM((2, 2 * block, width), BF16),
            pltpu.VMEM((2, LANES, width), BF16),
            plane,
            plane,
            plane,
            plane,
            plane,
            plane,
            plane,
            pltpu.VMEM((ROWS, width), F32),
            index,
            index,
            index,
            index,
            pltpu.VMEM((ROWS, coarse_padded), F32),
            pltpu.VMEM((ROWS, coarse_padded), F32),
            pltpu.VMEM((5, block, block), F32),
            pltpu.VMEM((halos, 4, block, width // 4), F32),
            pltpu.VMEM((halos, 4, block, width // 4), F32),
            held("sub", coarse_padded),
            held("seg", coarse_padded),
            held("sub", LANES),
            held("seg", LANES),
            dma((4,)),
            dma((halos, 2, 4)),
            held_sems("sub"),
            held_sems("seg"),
            held_sems("sub"),
            held_sems("seg"),
        ],
        compiler_params=pltpu.CompilerParams(
            collective_id=0, has_side_effects=True, vmem_limit_bytes=60 * 1024 * 1024
        ),
    )(
        face_len,
        primal_index,
        relax_step,
        nodal_loads,
        schur_matrix,
        face_rows,
        coarse_basis,
        coarse_inverse,
    )


def solution(mesh):
    placed = (
        P("seg", "sub", None, None),
        P("seg", "sub", None, None),
        P("seg", "sub", None),
        P(),
        P("seg", "sub"),
        P("seg", "sub", None, None),
        P(),
        P(),
    )
    return jax.shard_map(
        body,
        mesh=mesh,
        in_specs=placed,
        out_specs=(P("seg", "sub", None, None), P("seg", "sub", None, None)),
        check_vma=False,
    )
```

profile of v0, /device:TPU:0, one launch (start us, length us, event | category | flops | bytes accessed | tf_op | source)
XLA Modules:
  0.0 162.0 jit_solution(81804946457268669)
XLA Ops:
  1.3 1.4 copy.10.face_len
  2.7 1.4 copy.11.primal
  4.1 154.4 %shard_map.95 = (f32[1,1,32,3072]{3,2,1,0:T(8,128)}, f32[1,1,32,3072]{3,2,1,0:T(8,128)}) custom-call(s32[4,8,2]{2,1,0:T(8,128)} %copy.10.face_len, s32[4,8,4]{2,1,0:T(8,128)} %copy.11.primal, f32[1,1]{1,0:T(1,128)S(6)} %copy.14.relax_ref, f32[1,1,32,3072]{3,2,1,0:T(8,128)} %loads.1, bf16[1,1,3072,3072]{3,2,1,0:T(8,128)(2,1)} %schur.1, ...), custom_call_target="tpu_custom_call" | custom-call | tf_op jit(solution)/shard_map/pallas_call | solution.py:464
  158.4 1.8 %copy.15 = f32[1,1,32,3072]{3,2,1,0:T(8,128)} copy(f32[1,1,32,3072]{3,2,1,0:T(8,128)} %get-tuple-element.4) | data formatting | bytes 786432
  160.2 1.8 %copy.16 = f32[1,1,32,3072]{3,2,1,0:T(8,128)} copy(f32[1,1,32,3072]{3,2,1,0:T(8,128)} %get-tuple-element.5) | data formatting | bytes 786432
where the time goes:
time: 163 us; the launch traced here: 162 us
  Pallas kernels  154 us (94%)
  local copies, waits for them, and re-layouts  6.31 us (4%)
    pallas_call x1, Pallas kernels, body(): pl.pallas_call(functools.partial(solve_kernel, counts), out_shape=(out, o...  154 us
    unnamed x4, local copies, waits for them, and re-layouts  6.31 us

commit v1 on v0

--- a/solution.py
+++ b/solution.py
@@ -9,6 +9,7 @@
 
 DEG = 3
 ITERS = 3
+PIECES = 3
 
 HIGH = lax.Precision.HIGHEST
 MESH = pl.DeviceIdType.MESH
@@ -60,16 +61,21 @@
     coarse_rows,
     face_hot,
     small_state,
+    window,
     outgoing,
     incoming,
     coarse_first,
     coarse_second,
+    cross_first,
+    cross_second,
     inner_first,
     inner_second,
     load_sems,
     halo_sems,
     coarse_first_sems,
     coarse_second_sems,
+    cross_first_sems,
+    cross_second_sems,
     inner_first_sems,
     inner_second_sems,
 ):
@@ -104,28 +110,18 @@
         place_tile[d : d + 1] = row_tile[:, columns]
         place_lane[d : d + 1] = row_lane[:, columns]
 
-    def gathered(read, lane_ref, tile_ref, d):
+    def scan(read, lane_ref, tile_ref, d, sources, parts, base=0):
         lane = jnp.broadcast_to(lane_ref[pl.ds(d, 1)], (ROWS, LANES))
-        tile = jnp.broadcast_to(tile_ref[pl.ds(d, 1)], (ROWS, LANES))
-        parts = [jnp.zeros((ROWS, LANES), F32) for _ in range(groups)]
-        for s in range(tiles):
+        tile = jnp.broadcast_to(tile_ref[pl.ds(d, 1)] - base, (ROWS, LANES))
+        parts = list(parts)
+        for s in sources:
             hit = tile == s
             for g in range(groups):
                 moved = jnp.take_along_axis(
                     read(s, g), lane, axis=1, mode="promise_in_bounds"
                 )
                 parts[g] = jnp.where(hit, moved, parts[g])
-        return jnp.concatenate(parts, axis=0)
-
-    def pairs(count, visit):
-        unroll = 2 if count % 2 == 0 else 1
-
-        def step(i, _):
-            for u in range(unroll):
-                visit(i * unroll + u)
-            return 0
-
-        lax.fori_loop(0, count // unroll, step, 0)
+        return parts
 
     def part(g):
         return slice(g * ROWS, (g + 1) * ROWS)
@@ -140,44 +136,55 @@
         (2, 3, {"seg": peer("seg", -1)}),
     )
 
-    def halo_copies(e):
-        return [
-            pltpu.make_async_remote_copy(
-                src_ref=outgoing.at[e, face],
-                dst_ref=incoming.at[e, landing],
-                send_sem=halo_sems.at[e, 0, landing],
-                recv_sem=halo_sems.at[e, 1, landing],
-                device_id=target,
-                device_id_type=MESH,
-            )
-            for face, landing, target in routes
-        ]
-
-    def halo_start(e, read):
-        copies = halo_copies(e)
-        for (face, _, _), copy in zip(routes, copies):
-
-            def visit(d, face=face):
-                outgoing[e, face, :, span(d)] = gathered(
-                    read, place_lane, place_tile, d + face * face_tiles
+    def halo_copy(e, route):
+        face, landing, target = route
+        return pltpu.make_async_remote_copy(
+            src_ref=outgoing.at[e, face],
+            dst_ref=incoming.at[e, landing],
+            send_sem=halo_sems.at[e, 0, landing],
+            recv_sem=halo_sems.at[e, 1, landing],
+            device_id=target,
+            device_id_type=MESH,
+        )
+
+    def slots_of(e, source, sources, first, faces, base=0):
+        def read(s, g):
+            return source[part(g), s * LANES : (s + 1) * LANES]
+
+        for face in faces:
+            for q in range(face_tiles):
+                columns = slice(q * LANES, (q + 1) * LANES)
+                if first:
+                    parts = [jnp.zeros((ROWS, LANES), F32)] * groups
+                else:
+                    parts = [outgoing[e, face, part(g), columns] for g in range(groups)]
+                parts = scan(
+                    read, place_lane, place_tile, face * face_tiles + q, sources, parts, base
                 )
-
-            pairs(face_tiles, visit)
-            copy.start()
-
-    def halo_wait(e):
-        for copy in halo_copies(e):
-            copy.wait()
-
-    def halo_add(e, visit):
+                for g in range(groups):
+                    outgoing[e, face, part(g), columns] = parts[g]
+
+    def deliver(e, landings, visit):
+        for route in routes:
+            if route[1] in landings:
+                halo_copy(e, route).wait()
+
         def read(s, g):
             at = (s % face_tiles) * LANES
             return incoming[e, s // face_tiles, part(g), at : at + LANES]
 
-        def tile(d):
-            visit(span(d), gathered(read, back_lane, back_tile, d))
-
-        pairs(tiles, tile)
+        sources = [f * face_tiles + q for f in landings for q in range(face_tiles)]
+        unroll = tiles // 2
+
+        def step(i, _):
+            for u in range(unroll):
+                d = i * unroll + u
+                parts = [jnp.zeros((ROWS, LANES), F32)] * groups
+                parts = scan(read, back_lane, back_tile, d, sources, parts)
+                visit(span(d), jnp.concatenate(parts, axis=0))
+            return 0
+
+        lax.fori_loop(0, 2, step, 0)
 
     def sum_copy(axis, held, sems, r, d, landing):
         own = held.at[r, places[axis]]
@@ -191,7 +198,7 @@
         )
 
     def sum_start(axis, held, sems, r, value):
-        held[r, places[axis]] = value
+        held[r, places[axis], :, : value.shape[1]] = value
         for d in range(1, counts[axis]):
             sum_copy(axis, held, sems, r, d, False).start()
 
@@ -216,6 +223,41 @@
 
         lax.fori_loop(0, 2, column, 0)
 
+    pieces = PIECES if tiles % PIECES == 0 else 2
+    piece = tiles // pieces
+
+    def product_collect(source, visit, e, target):
+        def step(j, _):
+            before = jnp.maximum(j - 1, 0)
+            for q in range(piece):
+                window[:, q * LANES : (q + 1) * LANES] = target[:, span(before * piece + q)]
+            slots_of(e, window, range(piece), False, range(4), before * piece)
+            columns = pl.ds(pl.multiple_of(j * piece * LANES, LANES), piece * LANES)
+            both = jnp.dot(source[...], matrix[:, columns], preferred_element_type=F32)
+            visit(columns, both[:block] + both[block:])
+            return 0
+
+        lax.fori_loop(0, pieces, step, 0)
+
+    def collect_send(e, source, sources, first):
+        def step(a, _):
+            slots_of(e, source, sources, first, (2 * a + 1, 2 * a))
+            across = 1 - a
+            for shift in (1, -1):
+                target = {
+                    "sub": lax.rem(places["sub"] + across * shift + counts["sub"], counts["sub"]),
+                    "seg": lax.rem(places["seg"] + a * shift + counts["seg"], counts["seg"]),
+                }
+                landing = 2 * a + (0 if shift == 1 else 1)
+                face = 2 * a + (1 if shift == 1 else 0)
+                halo_copy(e, (face, landing, target)).start()
+            return 0
+
+        lax.fori_loop(0, 2, step, 0)
+
+    def collect_last(e, target):
+        collect_send(e, target, range(tiles - piece, tiles), False)
+
     def put_split(target, columns, values):
         upper, lower = split(values)
         target[:block, columns] = upper
@@ -224,7 +266,7 @@
     everything = slice(0, width)
 
     pl.semaphore_wait(barrier, len(greeted))
-    halo_start(0, lambda s, g: loads[0, 0, part(g), s * LANES : (s + 1) * LANES])
+    collect_send(0, loads.at[0, 0], range(tiles), True)
 
     padded_tiles = -(-tiles // 16) * 16
     at = lax.broadcasted_iota(jnp.int32, (padded_tiles, width), 0)
@@ -245,10 +287,10 @@
     seg_at, sub_at = places["seg"], places["sub"]
     seg_below = jnp.maximum(seg_at - 1, 0)
     lengths = (
-        face_len[seg_at, peer("sub", -1), 0],
-        face_len[seg_at, sub_at, 0],
-        jnp.where(seg_at > 0, face_len[seg_below, sub_at, 1], 0),
-        jnp.where(seg_at < counts["seg"] - 1, face_len[seg_at, sub_at, 1], 0),
+        face_len[seg_at, 0, peer("sub", -1)],
+        face_len[seg_at, 0, sub_at],
+        jnp.where(seg_at > 0, face_len[seg_below, 1, sub_at], 0),
+        jnp.where(seg_at < counts["seg"] - 1, face_len[seg_at, 1, sub_at], 0),
     )
     face_width = width // 4
     live = jnp.zeros(back.shape, jnp.bool_)
@@ -266,7 +308,7 @@
     coarse_padded = coarse_rows.shape[1]
     lane_at = lax.broadcasted_iota(jnp.int32, (1, coarse_padded), 1)
     hot = jnp.concatenate(
-        [jnp.where(lane_at == primal[seg_at, sub_at, f], 1.0, 0.0) for f in range(4)]
+        [jnp.where(lane_at == primal[seg_at, f, sub_at], 1.0, 0.0) for f in range(4)]
         + [jnp.zeros((ROWS - 4, coarse_padded), F32)],
         axis=0,
     )
@@ -296,34 +338,30 @@
             )
         return values
 
-    def mixed(left, right_ref):
-        upper, lower = split(left)
-        right_upper, right_lower = split(right_ref[...])
-        both = jnp.dot(
-            jnp.concatenate([upper, lower], axis=0), right_upper, preferred_element_type=F32
-        )
-        return both[:block] + both[block:] + jnp.dot(
-            upper, right_lower, preferred_element_type=F32
-        )
-
     direction[...] = jnp.zeros_like(direction)
     image[...] = jnp.zeros_like(image)
     solution[...] = jnp.zeros_like(solution)
     rights[...] = jnp.zeros_like(rights)
     small_state[...] = jnp.zeros_like(small_state)
 
-    halo_wait(0)
+    for held in (cross_first, cross_second, inner_first, inner_second):
+        for r in range(ITERS):
+            held[r] = jnp.zeros_like(held[r])
+    residual[...] = loads[...]
 
     def first_residual(columns, moved):
-        residual[0, 0, :, columns] = loads[0, 0, :, columns] + moved
-
-    halo_add(0, first_residual)
+        residual[0, 0, :, columns] = residual[0, 0, :, columns] + moved
+
+    for landings in ((2, 3), (0,), (1,)):
+        deliver(0, landings, first_residual)
     for fetch in fetches:
         fetch.wait()
 
+    def broad_weight(columns=slice(None)):
+        return jnp.concatenate([weight[:, columns]] * groups, axis=0)
+
     def round_of(r, _):
-        every_weight = jnp.concatenate([weight[...]] * groups, axis=0)
-        own_weighted = residual[0, 0] * every_weight
+        own_weighted = residual[0, 0] * broad_weight()
         weighted[...] = own_weighted
         own_scaled = relax * own_weighted
         scaled[...] = own_scaled
@@ -335,8 +373,7 @@
             terms = terms + local * face_hot[f : f + 1]
         sum_start("sub", coarse_first, coarse_first_sems, r, terms)
 
-        coarse_sum = None
-        for sweep in range(DEG):
+        for sweep in range(DEG - 1):
 
             def relaxed(columns, moved, sweep=sweep):
                 updated = scaled[:, columns] + state[:, columns] - relax * moved
@@ -347,69 +384,84 @@
             if sweep == 0:
                 terms = sum_finish("sub", coarse_first, coarse_first_sems, r)
                 sum_start("seg", coarse_second, coarse_second_sems, r, terms)
-            if sweep == DEG - 1:
-                coarse_sum = sum_finish("seg", coarse_second, coarse_second_sems, r)
-
-        corrected = state[...]
-        for f in range(4):
-            picked = jnp.sum(coarse_sum * coarse_rows[f : f + 1], axis=1, keepdims=True)
-            corrected = corrected + picked * basis_ref[0, 0, f : f + 1]
-        state[...] = corrected * jnp.concatenate([weight[...]] * groups, axis=0)
-        halo_start(1 + 2 * r, lambda s, g: state[part(g), s * LANES : (s + 1) * LANES])
+        coarse_sum = sum_finish("seg", coarse_second, coarse_second_sems, r)
+        picked = [
+            jnp.sum(coarse_sum * coarse_rows[f : f + 1], axis=1, keepdims=True)
+            for f in range(4)
+        ]
+
+        def corrected(columns, moved):
+            updated = scaled[:, columns] + state[:, columns] - relax * moved
+            for f in range(4):
+                updated = updated + picked[f] * basis_ref[0, 0, f : f + 1, columns]
+            state[:, columns] = updated * broad_weight(columns)
+
+        outward, inward = 1 + 2 * r, 2 + 2 * r
+        product_collect(lhs.at[(DEG - 1) % 2], corrected, outward, state)
+        collect_last(outward, state)
+
+        solution[0, 0] = solution[0, 0] + small(small_state[4], direction[...])
         small_state[0] = inverse_or_zero(r)
         put_split(rights_view(0), everything, weighted[...])
-        put_split(
-            rights_view(2),
-            everything,
-            image[...] * jnp.concatenate([weight[...]] * groups, axis=0),
-        )
-        halo_wait(1 + 2 * r)
+        put_split(rights_view(1), everything, image[...] * broad_weight())
 
         def joined(columns, moved):
+            state[:, columns] = state[:, columns] + moved
+
+        def joined_last(columns, moved):
             values = state[:, columns] + moved
             precond[:, columns] = values
             put_split(lhs.at[0], columns, values)
 
-        halo_add(1 + 2 * r, joined)
+        deliver(outward, (2, 3), joined)
+        deliver(outward, (0,), joined)
+        deliver(outward, (1,), joined_last)
+
+        def inner(rows):
+            both = sum(
+                lax.dot_general(lhs[0], rights[half, rows], NT, preferred_element_type=F32)
+                for half in range(2)
+            )
+            return both[:block] + both[block:]
+
+        sum_start("sub", cross_first, cross_first_sems, r, inner(slice(0, 2 * block)))
 
         def imaged(columns, moved):
             fresh[:, columns] = moved
-            put_split(rights_view(1), columns, moved)
-
-        product(lhs.at[0], imaged)
-        left = lhs[0]
-        both = lax.dot_general(left, rights[0], NT, preferred_element_type=F32)
-        both = both + lax.dot_general(left, rights[1], NT, preferred_element_type=F32)
-        sum_start("sub", inner_first, inner_first_sems, r, both[:block] + both[block:])
-        halo_start(2 + 2 * r, lambda s, g: fresh[part(g), s * LANES : (s + 1) * LANES])
+            put_split(rights_view(2), columns, moved)
+
+        product_collect(lhs.at[0], imaged, inward, fresh)
+        sum_start(
+            "sub", inner_first, inner_first_sems, r, inner(slice(2 * block, 3 * block))
+        )
+        terms = sum_finish("sub", cross_first, cross_first_sems, r)
+        sum_start("seg", cross_second, cross_second_sems, r, terms)
+        collect_last(inward, fresh)
+        sums = sum_finish("seg", cross_second, cross_second_sems, r)
+        rho = symmetric(sums[:, :block])
+        cross = pltpu.roll(sums, LANES - block, 1)[:, :block]
+        beta_t = small(rho, small_state[0])
+        old_part = 2.0 * small(cross, beta_t, NT) + small(
+            small(beta_t, small_state[2]), beta_t, NT
+        )
+        direction[...] = precond[...] + small(beta_t, direction[...])
+        image[...] = fresh[...] + small(beta_t, image[...])
         terms = sum_finish("sub", inner_first, inner_first_sems, r)
         sum_start("seg", inner_second, inner_second_sems, r, terms)
-        sums = sum_finish("seg", inner_second, inner_second_sems, r)
-        rho = symmetric(sums[:, :block])
-        own = pltpu.roll(sums, LANES - block, 1)[:, :block]
-        cross = pltpu.roll(sums, LANES - 2 * block, 1)[:, :block]
-        beta_t = small(rho, small_state[0])
-        curvature = symmetric(
-            own
-            + 2.0 * small(cross, beta_t, NT)
-            + small(small(beta_t, small_state[2]), beta_t, NT)
-        )
+
+        def added(columns, moved):
+            image[:, columns] = image[:, columns] + moved
+
+        deliver(inward, (2, 3), added)
+        own = sum_finish("seg", inner_second, inner_second_sems, r)[:, :block]
+        curvature = symmetric(own + old_part)
+        alpha_t = small(rho, inverse(curvature))
         small_state[1] = rho
         small_state[2] = curvature
-        alpha_t = small(rho, inverse(curvature))
-        small_state[3] = beta_t
         small_state[4] = alpha_t
-        direction[...] = precond[...] + mixed(beta_t, direction)
-        solution[0, 0] = solution[0, 0] + mixed(alpha_t, direction)
-        halo_wait(2 + 2 * r)
-        turned = mixed(beta_t, image)
-        image[...] = fresh[...] + turned
-
-        def added(columns, moved):
-            image[:, columns] = image[:, columns] + moved
-
-        halo_add(2 + 2 * r, added)
-        residual[0, 0] = residual[0, 0] - mixed(alpha_t, image)
+        deliver(inward, (0,), added)
+        deliver(inward, (1,), added)
+        residual[0, 0] = residual[0, 0] - small(alpha_t, image[...])
         return 0
 
     def rights_view(i):
@@ -421,6 +473,7 @@
         return jnp.where(first, 0.0, inverse(safe))
 
     lax.fori_loop(0, ITERS, round_of, 0)
+    solution[0, 0] = solution[0, 0] + small(small_state[4], direction[...])
 
 
 class _Rights:
@@ -478,7 +531,7 @@
         scratch_shapes=[
             pltpu.VMEM((width, width), BF16),
             pltpu.VMEM((2, 2 * block, width), BF16),
-            pltpu.VMEM((2, LANES, width), BF16),
+            pltpu.VMEM((2, 3 * block, width), BF16),
             plane,
             plane,
             plane,
@@ -494,14 +547,19 @@
             pltpu.VMEM((ROWS, coarse_padded), F32),
             pltpu.VMEM((ROWS, coarse_padded), F32),
             pltpu.VMEM((5, block, block), F32),
+            pltpu.VMEM((block, width // (PIECES if tiles % PIECES == 0 else 2)), F32),
             pltpu.VMEM((halos, 4, block, width // 4), F32),
             pltpu.VMEM((halos, 4, block, width // 4), F32),
             held("sub", coarse_padded),
             held("seg", coarse_padded),
             held("sub", LANES),
             held("seg", LANES),
+            held("sub", LANES),
+            held("seg", LANES),
             dma((4,)),
             dma((halos, 2, 4)),
+            held_sems("sub"),
+            held_sems("seg"),
             held_sems("sub"),
             held_sems("seg"),
             held_sems("sub"),
@@ -511,8 +569,8 @@
             collective_id=0, has_side_effects=True, vmem_limit_bytes=60 * 1024 * 1024
         ),
     )(
-        face_len,
-        primal_index,
+        face_len.transpose(0, 2, 1),
+        primal_index.transpose(0, 2, 1),
         relax_step,
         nodal_loads,
         schur_matrix,

time: 163 us -> 143 us (0.88)
  Pallas kernels: 154 us -> 138 us
  local copies, waits for them, and re-layouts: 6.31 us -> 3.53 us
    pallas_call x1, Pallas kernels: 154 us -> 138 us  [body(): pl.pallas_call(functools.partial(solve_kernel, counts), out_shape=(out, o...]
    unnamed x4 -> x2, local copies, waits for them, and re-layouts: 6.31 us -> 3.53 us
where the time goes in v1:
time: 143 us
  Pallas kernels  138 us (97%)
  local copies, waits for them, and re-layouts  3.53 us (2%)
    pallas_call x1, Pallas kernels, body(): pl.pallas_call(functools.partial(solve_kernel, counts), out_shape=(out, o...  138 us
    unnamed x2, local copies, waits for them, and re-layouts  3.53 us

profile of v1, /device:TPU:0, one launch (start us, length us, event | category | flops | bytes accessed | tf_op | source)
XLA Modules:
  0.0 142.9 jit_solution(6860679514420490014)
XLA Ops:
  1.3 138.1 %shard_map.95 = (f32[1,1,32,3072]{3,2,1,0:T(8,128)}, f32[1,1,32,3072]{3,2,1,0:T(8,128)}) custom-call(s32[4,2,8]{2,1,0:T(2,128)} %bitcast.3, s32[4,4,8]{2,1,0:T(4,128)} %bitcast.2, f32[1,1]{1,0:T(1,128)S(6)} %copy.12.relax_ref, f32[1,1,32,3072]{3,2,1,0:T(8,128)} %loads.1, bf16[1,1,3072,3072]{3,2,1,0:T(8,128)(2,1)} %schur.1, s32[1,1,3072]{2,1,0:T(1,128)} %rows_ref.1, ...), custom_call_target="tpu_custom_call" | custom-call | tf_op jit(solution)/shard_map/pallas_call | solution.py:517
  139.4 1.8 %copy.13 = f32[1,1,32,3072]{3,2,1,0:T(8,128)} copy(f32[1,1,32,3072]{3,2,1,0:T(8,128)} %get-tuple-element.4) | data formatting | bytes 786432
  141.1 1.8 %copy.14 = f32[1,1,32,3072]{3,2,1,0:T(8,128)} copy(f32[1,1,32,3072]{3,2,1,0:T(8,128)} %get-tuple-element.5) | data formatting | bytes 786432

commit v2 on v1

--- a/solution.py
+++ b/solution.py
@@ -61,6 +61,10 @@
     coarse_rows,
     face_hot,
     small_state,
+    picked,
+    packing,
+    basis_weighted,
+    basis_slots,
     window,
     outgoing,
     incoming,
@@ -116,7 +120,7 @@
         parts = list(parts)
         for s in sources:
             hit = tile == s
-            for g in range(groups):
+            for g in range(len(parts)):
                 moved = jnp.take_along_axis(
                     read(s, g), lane, axis=1, mode="promise_in_bounds"
                 )
@@ -147,7 +151,7 @@
             device_id_type=MESH,
         )
 
-    def slots_of(e, source, sources, first, faces, base=0):
+    def slots_of(e, source, sources, first, faces, base=0, finish=None):
         def read(s, g):
             return source[part(g), s * LANES : (s + 1) * LANES]
 
@@ -161,10 +165,12 @@
                 parts = scan(
                     read, place_lane, place_tile, face * face_tiles + q, sources, parts, base
                 )
+                if finish is not None:
+                    parts = finish(span(face * face_tiles + q), parts)
                 for g in range(groups):
                     outgoing[e, face, part(g), columns] = parts[g]
 
-    def deliver(e, landings, visit):
+    def deliver(e, landings, visit, loop=True):
         for route in routes:
             if route[1] in landings:
                 halo_copy(e, route).wait()
@@ -174,17 +180,32 @@
             return incoming[e, s // face_tiles, part(g), at : at + LANES]
 
         sources = [f * face_tiles + q for f in landings for q in range(face_tiles)]
-        unroll = tiles // 2
+        unroll = tiles // 2 if loop else tiles
 
         def step(i, _):
             for u in range(unroll):
                 d = i * unroll + u
                 parts = [jnp.zeros((ROWS, LANES), F32)] * groups
                 parts = scan(read, back_lane, back_tile, d, sources, parts)
-                visit(span(d), jnp.concatenate(parts, axis=0))
+                columns = span(d) if loop else slice(d * LANES, (d + 1) * LANES)
+                visit(columns, jnp.concatenate(parts, axis=0))
             return 0
 
-        lax.fori_loop(0, 2, step, 0)
+        if loop:
+            lax.fori_loop(0, 2, step, 0)
+        else:
+            step(0, 0)
+
+    def packed(values):
+        packing[:, :block] = values
+        tile = packing[part(0)]
+        for g in range(1, groups):
+            tile = tile + pltpu.roll(packing[part(g)], g * block, 1)
+        return tile
+
+    def unpacked(tile):
+        rolled = [tile] + [pltpu.roll(tile, LANES - g * block, 1) for g in range(1, groups)]
+        return jnp.concatenate([rows[:, :block] for rows in rolled], axis=0)
 
     def sum_copy(axis, held, sems, r, d, landing):
         own = held.at[r, places[axis]]
@@ -198,7 +219,7 @@
         )
 
     def sum_start(axis, held, sems, r, value):
-        held[r, places[axis], :, : value.shape[1]] = value
+        held[r, places[axis]] = value
         for d in range(1, counts[axis]):
             sum_copy(axis, held, sems, r, d, False).start()
 
@@ -239,9 +260,9 @@
 
         lax.fori_loop(0, pieces, step, 0)
 
-    def collect_send(e, source, sources, first):
+    def collect_send(e, source, sources, first, finish=None):
         def step(a, _):
-            slots_of(e, source, sources, first, (2 * a + 1, 2 * a))
+            slots_of(e, source, sources, first, (2 * a + 1, 2 * a), finish=finish)
             across = 1 - a
             for shift in (1, -1):
                 target = {
@@ -255,8 +276,8 @@
 
         lax.fori_loop(0, 2, step, 0)
 
-    def collect_last(e, target):
-        collect_send(e, target, range(tiles - piece, tiles), False)
+    def collect_last(e, target, finish=None):
+        collect_send(e, target, range(tiles - piece, tiles), False, finish)
 
     def put_split(target, columns, values):
         upper, lower = split(values)
@@ -344,9 +365,23 @@
     rights[...] = jnp.zeros_like(rights)
     small_state[...] = jnp.zeros_like(small_state)
 
-    for held in (cross_first, cross_second, inner_first, inner_second):
-        for r in range(ITERS):
-            held[r] = jnp.zeros_like(held[r])
+    packing[...] = jnp.zeros_like(packing)
+    basis_weighted[...] = jnp.zeros_like(basis_weighted)
+    basis_weighted[:4] = basis_ref[0, 0] * weight[:4]
+
+    def basis_tile(d, _):
+        parts = scan(
+            lambda s, g: basis_weighted[:, s * LANES : (s + 1) * LANES],
+            place_lane,
+            place_tile,
+            d,
+            range(tiles),
+            [jnp.zeros((ROWS, LANES), F32)],
+        )
+        basis_slots[:, span(d)] = parts[0]
+        return 0
+
+    lax.fori_loop(0, tiles, basis_tile, 0)
     residual[...] = loads[...]
 
     def first_residual(columns, moved):
@@ -361,49 +396,70 @@
         return jnp.concatenate([weight[:, columns]] * groups, axis=0)
 
     def round_of(r, _):
-        own_weighted = residual[0, 0] * broad_weight()
-        weighted[...] = own_weighted
-        own_scaled = relax * own_weighted
-        scaled[...] = own_scaled
-        state[...] = own_scaled
-        put_split(lhs.at[0], everything, own_scaled)
+        sums = [jnp.zeros((block, LANES), F32)] * 4
+        for d in range(tiles):
+            columns = slice(d * LANES, (d + 1) * LANES)
+            own_weighted = residual[0, 0, :, columns] * broad_weight(columns)
+            weighted[:, columns] = own_weighted
+            own_scaled = relax * own_weighted
+            scaled[:, columns] = own_scaled
+            put_split(lhs.at[0], columns, own_scaled)
+            for f in range(4):
+                sums[f] = sums[f] + own_weighted * basis_ref[0, 0, f : f + 1, columns]
         terms = jnp.zeros((block, coarse_padded), F32)
         for f in range(4):
-            local = jnp.sum(own_weighted * basis_ref[0, 0, f : f + 1], axis=1, keepdims=True)
+            local = jnp.sum(sums[f], axis=1, keepdims=True)
             terms = terms + local * face_hot[f : f + 1]
         sum_start("sub", coarse_first, coarse_first_sems, r, terms)
 
         for sweep in range(DEG - 1):
 
             def relaxed(columns, moved, sweep=sweep):
-                updated = scaled[:, columns] + state[:, columns] - relax * moved
+                before = state if sweep else scaled
+                updated = scaled[:, columns] + before[:, columns] - relax * moved
                 state[:, columns] = updated
                 put_split(lhs.at[(sweep + 1) % 2], columns, updated)
 
             product(lhs.at[sweep % 2], relaxed)
-            if sweep == 0:
-                terms = sum_finish("sub", coarse_first, coarse_first_sems, r)
-                sum_start("seg", coarse_second, coarse_second_sems, r, terms)
+        terms = sum_finish("sub", coarse_first, coarse_first_sems, r)
+        sum_start("seg", coarse_second, coarse_second_sems, r, terms)
+
+        def swept(columns, moved):
+            updated = scaled[:, columns] + state[:, columns] - relax * moved
+            state[:, columns] = updated * broad_weight(columns)
+
+        outward, inward = 1 + 2 * r, 2 + 2 * r
+        product_collect(lhs.at[(DEG - 1) % 2], swept, outward, state)
         coarse_sum = sum_finish("seg", coarse_second, coarse_second_sems, r)
-        picked = [
-            jnp.sum(coarse_sum * coarse_rows[f : f + 1], axis=1, keepdims=True)
-            for f in range(4)
-        ]
-
-        def corrected(columns, moved):
-            updated = scaled[:, columns] + state[:, columns] - relax * moved
+        for f in range(4):
+            picked[f] = jnp.broadcast_to(
+                jnp.sum(coarse_sum * coarse_rows[f : f + 1], axis=1, keepdims=True),
+                (block, LANES),
+            )
+
+        def corrected(parts, rows):
             for f in range(4):
-                updated = updated + picked[f] * basis_ref[0, 0, f : f + 1, columns]
-            state[:, columns] = updated * broad_weight(columns)
-
-        outward, inward = 1 + 2 * r, 2 + 2 * r
-        product_collect(lhs.at[(DEG - 1) % 2], corrected, outward, state)
-        collect_last(outward, state)
+                row = jnp.broadcast_to(rows[f : f + 1], (ROWS, LANES))
+                parts = [parts[g] + picked[f, part(g)] * row for g in range(groups)]
+            return parts
+
+        collect_last(
+            outward, state, lambda columns, parts: corrected(parts, basis_slots[:, columns])
+        )
+        for d in range(tiles):
+            columns = slice(d * LANES, (d + 1) * LANES)
+            parts = corrected(
+                [state[part(g), columns] for g in range(groups)], basis_weighted[:, columns]
+            )
+            for g in range(groups):
+                state[part(g), columns] = parts[g]
 
         solution[0, 0] = solution[0, 0] + small(small_state[4], direction[...])
         small_state[0] = inverse_or_zero(r)
-        put_split(rights_view(0), everything, weighted[...])
-        put_split(rights_view(1), everything, image[...] * broad_weight())
+        for d in range(tiles):
+            columns = slice(d * LANES, (d + 1) * LANES)
+            put_split(rights_view(0), columns, weighted[:, columns])
+            put_split(rights_view(1), columns, image[:, columns] * broad_weight(columns))
 
         def joined(columns, moved):
             state[:, columns] = state[:, columns] + moved
@@ -414,8 +470,7 @@
             put_split(lhs.at[0], columns, values)
 
         deliver(outward, (2, 3), joined)
-        deliver(outward, (0,), joined)
-        deliver(outward, (1,), joined_last)
+        deliver(outward, (0, 1), joined_last)
 
         def inner(rows):
             both = sum(
@@ -424,22 +479,29 @@
             )
             return both[:block] + both[block:]
 
-        sum_start("sub", cross_first, cross_first_sems, r, inner(slice(0, 2 * block)))
+        sum_start(
+            "sub",
+            cross_first,
+            cross_first_sems,
+            r,
+            jnp.concatenate(
+                [packed(inner(slice(i * block, (i + 1) * block))) for i in range(2)], axis=0
+            ),
+        )
 
         def imaged(columns, moved):
             fresh[:, columns] = moved
             put_split(rights_view(2), columns, moved)
 
         product_collect(lhs.at[0], imaged, inward, fresh)
-        sum_start(
-            "sub", inner_first, inner_first_sems, r, inner(slice(2 * block, 3 * block))
-        )
         terms = sum_finish("sub", cross_first, cross_first_sems, r)
         sum_start("seg", cross_second, cross_second_sems, r, terms)
+        own_terms = packed(inner(slice(2 * block, 3 * block)))
+        sum_start("sub", inner_first, inner_first_sems, r, own_terms)
         collect_last(inward, fresh)
         sums = sum_finish("seg", cross_second, cross_second_sems, r)
-        rho = symmetric(sums[:, :block])
-        cross = pltpu.roll(sums, LANES - block, 1)[:, :block]
+        rho = symmetric(unpacked(sums[:ROWS]))
+        cross = unpacked(sums[ROWS:])
         beta_t = small(rho, small_state[0])
         old_part = 2.0 * small(cross, beta_t, NT) + small(
             small(beta_t, small_state[2]), beta_t, NT
@@ -453,14 +515,13 @@
             image[:, columns] = image[:, columns] + moved
 
         deliver(inward, (2, 3), added)
-        own = sum_finish("seg", inner_second, inner_second_sems, r)[:, :block]
+        own = unpacked(sum_finish("seg", inner_second, inner_second_sems, r))
+        deliver(inward, (0, 1), added, loop=False)
         curvature = symmetric(own + old_part)
         alpha_t = small(rho, inverse(curvature))
         small_state[1] = rho
         small_state[2] = curvature
         small_state[4] = alpha_t
-        deliver(inward, (0,), added)
-        deliver(inward, (1,), added)
         residual[0, 0] = residual[0, 0] - small(alpha_t, image[...])
         return 0
 
@@ -505,8 +566,8 @@
     index = pltpu.VMEM((tiles, LANES), jnp.int32)
     dma = pltpu.SemaphoreType.DMA
 
-    def held(axis, columns):
-        return pltpu.VMEM((ITERS, counts[axis], block, columns), F32)
+    def held(axis, rows, columns=LANES):
+        return pltpu.VMEM((ITERS, counts[axis], rows, columns), F32)
 
     def held_sems(axis):
         return dma((ITERS, 2, counts[axis]))
@@ -547,15 +608,19 @@
             pltpu.VMEM((ROWS, coarse_padded), F32),
             pltpu.VMEM((ROWS, coarse_padded), F32),
             pltpu.VMEM((5, block, block), F32),
+            pltpu.VMEM((4, block, LANES), F32),
+            pltpu.VMEM((block, LANES), F32),
+            pltpu.VMEM((ROWS, width), F32),
+            pltpu.VMEM((ROWS, width), F32),
             pltpu.VMEM((block, width // (PIECES if tiles % PIECES == 0 else 2)), F32),
             pltpu.VMEM((halos, 4, block, width // 4), F32),
             pltpu.VMEM((halos, 4, block, width // 4), F32),
-            held("sub", coarse_padded),
-            held("seg", coarse_padded),
-            held("sub", LANES),
-            held("seg", LANES),
-            held("sub", LANES),
-            held("seg", LANES),
+            held("sub", block, coarse_padded),
+            held("seg", block, coarse_padded),
+            held("sub", 2 * ROWS),
+            held("seg", 2 * ROWS),
+            held("sub", ROWS),
+            held("seg", ROWS),
             dma((4,)),
             dma((halos, 2, 4)),
             held_sems("sub"),

time: 143 us -> 133 us (0.930)
  Pallas kernels: 138 us -> 128 us
    pallas_call x1, Pallas kernels: 138 us -> 128 us  [body(): pl.pallas_call(functools.partial(solve_kernel, counts), out_shape=(out, o...]
where the time goes in v2:
time: 133 us; the launch traced here: 132 us
  Pallas kernels  128 us (96%)
  local copies, waits for them, and re-layouts  3.53 us (3%)
    pallas_call x1, Pallas kernels, body(): pl.pallas_call(functools.partial(solve_kernel, counts), out_shape=(out, o...  128 us
    unnamed x2, local copies, waits for them, and re-layouts  3.53 us

profile of v2, /device:TPU:0, one launch (start us, length us, event | category | flops | bytes accessed | tf_op | source)
XLA Modules:
  0.0 132.4 jit_solution(17868735005325604837)
XLA Ops:
  1.3 127.6 %shard_map.95 = (f32[1,1,32,3072]{3,2,1,0:T(8,128)}, f32[1,1,32,3072]{3,2,1,0:T(8,128)}) custom-call(s32[4,2,8]{2,1,0:T(2,128)} %bitcast.3, s32[4,4,8]{2,1,0:T(4,128)} %bitcast.2, f32[1,1]{1,0:T(1,128)S(6)} %copy.12.relax_ref, f32[1,1,32,3072]{3,2,1,0:T(8,128)} %loads.1, bf16[1,1,3072,3072]{3,2,1,0:T(8,128)(2,1)} %schur.1, s32[1,1,3072]{2,1,0:T(1,128)} %rows_ref.1, ...), custom_call_target="tpu_custom_call" | custom-call | tf_op jit(solution)/shard_map/pallas_call | solution.py:578
  128.9 1.8 %copy.13 = f32[1,1,32,3072]{3,2,1,0:T(8,128)} copy(f32[1,1,32,3072]{3,2,1,0:T(8,128)} %get-tuple-element.4) | data formatting | bytes 786432
  130.7 1.8 %copy.14 = f32[1,1,32,3072]{3,2,1,0:T(8,128)} copy(f32[1,1,32,3072]{3,2,1,0:T(8,128)} %get-tuple-element.5) | data formatting | bytes 786432

commit v3 on v2

--- a/solution.py
+++ b/solution.py
@@ -387,7 +387,7 @@
     def first_residual(columns, moved):
         residual[0, 0, :, columns] = residual[0, 0, :, columns] + moved
 
-    for landings in ((2, 3), (0,), (1,)):
+    for landings in ((2, 3), (0, 1)):
         deliver(0, landings, first_residual)
     for fetch in fetches:
         fetch.wait()
@@ -575,7 +575,7 @@
     out = jax.ShapeDtypeStruct(nodal_loads.shape, F32)
     smem = pl.BlockSpec(memory_space=pltpu.SMEM)
     vmem = pl.BlockSpec(memory_space=pltpu.VMEM)
-    return pl.pallas_call(
+    solved = pl.pallas_call(
         functools.partial(solve_kernel, counts),
         out_shape=(out, out),
         in_specs=[
@@ -643,6 +643,14 @@
         coarse_basis,
         coarse_inverse,
     )
+    return pl.pallas_call(
+        hand_over, out_shape=(out, out), in_specs=[vmem, vmem], out_specs=(vmem, vmem)
+    )(*solved)
+
+
+def hand_over(solved, left, solution, residual):
+    solution[...] = solved[...]
+    residual[...] = left[...]
 
 
 def solution(mesh):

time: 133 us -> 131 us (0.985)
  local copies, waits for them, and re-layouts: 3.53 us -> 0 us
    unnamed x2 -> x0, local copies, waits for them, and re-layouts: 3.53 us -> none
    pallas_call x0 -> x1, Pallas kernels: none -> 2.02 us  [body(): pl.pallas_call(hand_over, out_shape=(out, out), in_specs=[vmem, vmem], ou...]
where the time goes in v3:
time: 131 us
  Pallas kernels  129 us (98%)
    pallas_call x1, Pallas kernels, body(): pl.pallas_call(functools.partial(solve_kernel, counts), out_shape=(out, o...  127 us

profile of v3, /device:TPU:0, one launch (start us, length us, event | category | flops | bytes accessed | tf_op | source)
XLA Modules:
  0.0 130.7 jit_solution(11638500640557074613)
XLA Ops:
  1.3 127.4 %shard_map.95 = (f32[1,1,32,3072]{3,2,1,0:T(8,128)}, f32[1,1,32,3072]{3,2,1,0:T(8,128)}) custom-call(s32[4,2,8]{2,1,0:T(2,128)} %bitcast.3, s32[4,4,8]{2,1,0:T(4,128)} %bitcast.2, f32[1,1]{1,0:T(1,128)S(6)} %copy.10.relax_ref, f32[1,1,32,3072]{3,2,1,0:T(8,128)} %loads.1, bf16[1,1,3072,3072]{3,2,1,0:T(8,128)(2,1)} %schur.1, s32[1,1,3072]{2,1,0:T(1,128)} %rows_ref.1, ...), custom_call_target="tpu_custom_call" | custom-call | tf_op jit(solution)/shard_map/pallas_call | solution.py:578
  128.7 2.0 %shard_map.96 = (f32[1,1,32,3072]{3,2,1,0:T(8,128)}, f32[1,1,32,3072]{3,2,1,0:T(8,128)}) custom-call(f32[1,1,32,3072]{3,2,1,0:T(8,128)} %get-tuple-element.4.solved, f32[1,1,32,3072]{3,2,1,0:T(8,128)} %get-tuple-element.5.left), custom_call_target="tpu_custom_call" | custom-call | tf_op jit(solution)/shard_map/pallas_call | solution.py:646
